TPU v7x, 32 devices: a whole 2x2x4 slice. The times are simulated.
32 devices in a mesh: groups: 2 (over y), filt: 4 (over z), sp: 2 (over x), in: 2 (over core).
Axes of the slice: x: 2, y: 2, z: 4, core: 2. Of those that a mesh axis runs over, the one named last changes fastest.
Arguments:
- image: bfloat16 [16, 256, 1024], P(('groups', 'sp', 'filt'), None, 'in'), parts along dimension 0, may hold values from -6 to 6
- weight: bfloat16 [3, 3, 1024, 1024], P(None, None, 'filt'), may hold values from -0.0625 to 0.0625
- bias: float32 [1024], P('filt'), may hold values from -3 to 3
- cotangent: bfloat16 [16, 1024, 256], P(('groups', 'sp'), 'filt'), parts along dimension 0, may hold values from -0.029907227 to 0.029907227
Outputs:
- output: bfloat16 [16, 1024, 256], P(('groups', 'sp', 'filt'), None, 'in'), parts along dimension 0
- grad_weight: float32 [6, 3, 1024, 1024], P('groups', None, 'filt', 'in'), parts along dimension 0
- grad_bias: float32 [2048], P(('groups', 'filt')), parts along dimension 0
There are 2 independent parts, one for each index of `groups`. A program takes and returns all parts, laid end to end along the dimension named above; an argument that names none is the same for every part. Nothing has to cross between parts.
All inputs are finite; a program needn't handle non-finite values.
Results may differ from a plain program's by a relative error of at most 0.0055.
Values may be sent and summed in bfloat16 or wider, within the bound.
A program may use at most 64 MiB of HBM per device.

v0:
```python
import functools

import jax
import jax.numpy as jnp
from jax import lax
from jax.experimental import pallas as pl
from jax.experimental.pallas import tpu as pltpu
from jax.sharding import PartitionSpec as P

MESH = pl.DeviceIdType.MESH
NT = (((1,), (1,)), ((), ()))


def shift_cols(value, by):
    cols = value.shape[1]
    col = lax.broadcasted_iota(jnp.int32, value.shape, 1)
    if by < 0:
        return jnp.where(col == 0, 0.0, pltpu.roll(value, 1, 1))
    return jnp.where(col == cols - 1, 0.0, pltpu.roll(value, cols - 1, 1))


def lanes(q, cols, count=1):
    return pl.ds(pl.multiple_of(q * cols, cols), count * cols)


def store_shifts(grads, place, grad):
    wide = grad.astype(jnp.float32)
    grads[0, :, place] = shift_cols(wide, 1).astype(jnp.bfloat16)
    grads[2, :, place] = shift_cols(wide, -1).astype(jnp.bfloat16)


def rows_tap(rows, grads, a, b, start, count):
    cols, depth = rows.shape[1], rows.shape[2]
    window = rows[pl.ds(start + a, count)].reshape(count * cols, depth)
    return jnp.dot(
        grads[b, :, lanes(start, cols, count)], window, preferred_element_type=jnp.float32
    )


def late_row(block, n_f):
    return block * n_f + jnp.where(block > 0, 0, n_f - 1)


def early_row(block, n_f):
    return block * n_f + jnp.where(block > 0, 1, 0)


def gather_kernel(
    n_f, n_s,
    image, weight, bias_in, cotangent,
    rows, grads, gw_own, out,
    w, bias, cot, part, peer, act,
    load_sem, row_send, row_recv, x_send, sum_send, sum_recv,
    g_send, g_recv, h_send, h_recv, out_send, out_recv,
):
    p, s, c = lax.axis_index("filt"), lax.axis_index("sp"), lax.axis_index("in")
    sibling = 1 - c
    cols, depth = rows.shape[1], rows.shape[2]
    o = w.shape[2]
    half_c = out.shape[1]
    total = n_f * n_s
    first = s * n_f
    last = n_f - 1
    x_peers = [lax.rem(s + d, n_s) for d in range(1, n_s)]

    load_row = pltpu.make_async_copy(image.at[0], rows.at[1 + first + p], load_sem.at[0])
    load_w = pltpu.make_async_copy(
        weight.at[:, :, :, pl.ds(pl.multiple_of(c * depth, depth), depth)], w, load_sem.at[1]
    )
    load_cot = pltpu.make_async_copy(cotangent, cot, load_sem.at[2])
    load_bias = pltpu.make_async_copy(bias_in, bias, load_sem.at[3])
    load_row.start()
    load_w.start()
    load_cot.start()
    load_bias.start()

    barrier = pltpu.get_barrier_semaphore()
    for d in range(1, n_f):
        pl.semaphore_signal(barrier, 1, device_id={"filt": lax.rem(p + d, n_f)}, device_id_type=MESH)
    for peer_s in x_peers:
        pl.semaphore_signal(barrier, 1, device_id={"sp": peer_s}, device_id_type=MESH)
    pl.semaphore_signal(barrier, 1, device_id={"in": sibling}, device_id_type=MESH)
    pl.semaphore_wait(barrier, n_f - 1 + n_s - 1 + 1)

    piece = cols // 2

    def row_copy(q, h, way, where, send):
        slot = rows.at[1 + q, pl.ds(h * piece, piece)]
        return pltpu.make_async_remote_copy(
            src_ref=slot, dst_ref=slot, send_sem=send, recv_sem=row_recv.at[q, h],
            device_id={way: where}, device_id_type=MESH,
        )

    def to_right(q, h):
        return row_copy(q, h, "filt", p + 1, row_send.at[0, q, h])

    def to_left(q, h):
        return row_copy(q, h, "filt", p - 1, row_send.at[1, q, h])

    def to_x(q, h, d):
        return row_copy(first + q, h, "sp", x_peers[d], x_send.at[d, q, h])

    def wait_row(q, h):
        row_copy(q, h, "filt", p, row_send.at[0, 0, 0]).wait_recv()

    def crosses(q):
        return ((q > 0) & (q < last)) | (q == p)

    def pass_on(q, h, right, left):
        if right:
            @pl.when(p < last)
            def _():
                to_right(first + q, h).start()
        if left:
            @pl.when(p > 0)
            def _():
                to_left(first + q, h).start()

        @pl.when(crosses(q))
        def _():
            for d in range(n_s - 1):
                to_x(q, h, d).start()

    load_row.wait()
    for h in range(2):
        pass_on(p, h, True, True)

    zero = jnp.zeros((cols, depth), rows.dtype)
    rows[0] = zero
    rows[total + 1] = zero

    @pl.loop(0, n_f + 2)
    def _(r):
        part[r] = jnp.zeros((o, cols), jnp.float32)

    load_w.wait()

    def add_tap(q, a, r):
        sums = lax.dot_general(
            w[a].reshape(3 * o, depth), rows[1 + q], NT, preferred_element_type=jnp.float32
        )
        part[r + 1] += shift_cols(sums[:o], -1) + sums[o:2 * o] + shift_cols(sums[2 * o:], 1)

    def add_row(q):
        for a in range(3):
            add_tap(first + q, a, q - a + 1)

    def sum_copy(r):
        return pltpu.make_async_remote_copy(
            src_ref=part.at[r + 1], dst_ref=peer.at[r], send_sem=sum_send.at[r], recv_sem=sum_recv.at[r],
            device_id={"in": sibling}, device_id_type=MESH,
        )

    def out_copy(r):
        return pltpu.make_async_remote_copy(
            src_ref=act.at[r, :, pl.ds(pl.multiple_of(c * half_c, half_c), half_c)],
            dst_ref=out.at[pl.ds(pl.multiple_of(p * o, o), o), :],
            send_sem=out_send.at[r], recv_sem=out_recv.at[p],
            device_id={"filt": r}, device_id_type=MESH,
        )

    own_out = pltpu.make_async_copy(
        act.at[p, :, pl.ds(pl.multiple_of(c * half_c, half_c), half_c)],
        out.at[pl.ds(pl.multiple_of(p * o, o), o), :],
        load_sem.at[0],
    )

    half_o = o // 2

    def g_half(q, core):
        return grads.at[1, pl.ds(pl.multiple_of(core * half_o, half_o), half_o), lanes(q, cols)]

    def g_copy(q, d):
        place = g_half(q, c)
        return pltpu.make_async_remote_copy(
            src_ref=place, dst_ref=place, send_sem=g_send.at[d, q], recv_sem=g_recv.at[q],
            device_id={"sp": x_peers[d]}, device_id_type=MESH,
        )

    def h_copy(q, core):
        place = g_half(q, core)
        return pltpu.make_async_remote_copy(
            src_ref=place, dst_ref=place, send_sem=h_send.at[q], recv_sem=h_recv.at[q],
            device_id={"in": sibling}, device_id_type=MESH,
        )

    def done_at(r):
        low = jnp.where(s == 0, jnp.maximum(p, 1), jnp.maximum(p, n_f - p))
        high = jnp.where(
            s == n_s - 1, jnp.maximum(last - p, 1), jnp.maximum(last - p, p + 1)
        )
        return jnp.where(r == 0, low, jnp.where(r == last, high, jnp.abs(r - p) + 1))

    def finish(r):
        sum_copy(r).wait_recv()
        bias_all = jnp.broadcast_to(bias[...], (cols, o)).T
        shifted = part[r + 1] + peer[r] + bias_all
        sig = jax.nn.sigmoid(shifted)
        slope = sig * (1.0 + shifted * (1.0 - sig))
        grad = (cot[r].astype(jnp.float32) * slope).astype(jnp.bfloat16)
        place = lanes(first + r, cols)
        grads[1, :, place] = grad
        act[r] = (shifted * sig).astype(jnp.bfloat16)
        for d in range(n_s - 1):
            g_copy(first + r, d).start()

        store_shifts(grads, place, grad)

    def send_out(r):
        @pl.when(r == p)
        def _():
            own_out.start()

        @pl.when(r != p)
        def _():
            out_copy(r).start()

    add_row(p)
    load_cot.wait()
    load_bias.wait()

    def relay(t):
        @pl.when(t == p + 1)
        def _():
            for block in x_peers:
                for h in range(2):
                    wait_row(block * n_f, h)

                    @pl.when(p < last)
                    def _():
                        to_right(block * n_f, h).start()

        @pl.when(t == n_f - p)
        def _():
            for block in x_peers:
                for h in range(2):
                    wait_row(block * n_f + last, h)

                    @pl.when(p > 0)
                    def _():
                        to_left(block * n_f + last, h).start()

    def add_edges(t):
        @pl.when((t == p + 1) & (s < n_s - 1))
        def _():
            add_tap(first + n_f, 2, last)

        @pl.when((t == n_f - p) & (s > 0))
        def _():
            add_tap(first - 1, 0, 0)

    def start_sums(t):
        @pl.loop(0, n_f)
        def _(r):
            @pl.when(done_at(r) == t)
            def _():
                sum_copy(r).start()

    def finish_rows(t):
        @pl.loop(0, n_f)
        def _(r):
            @pl.when(done_at(r) == t)
            def _():
                finish(r)

    @pl.loop(1, n_f)
    def _(t):
        for h in range(2):
            @pl.when(p - t >= 0)
            def _():
                wait_row(first + p - t, h)
                pass_on(p - t, h, True, False)

            @pl.when(p + t < n_f)
            def _():
                wait_row(first + p + t, h)
                pass_on(p + t, h, False, True)

        relay(t)

        @pl.when(p - t >= 0)
        def _():
            add_row(p - t)

        @pl.when(p + t < n_f)
        def _():
            add_row(p + t)

        add_edges(t)
        start_sums(t)
        finish_rows(t - 1)

    def own_rows():
        @pl.loop(0, 9)
        def _(k):
            gw_own[k] = rows_tap(rows, grads, k // 3, lax.rem(k, 3), early_row(s, n_f), n_f - 1)

    finish_rows(n_f - 1)
    if n_s <= 2:
        own_rows()
    relay(n_f)
    add_edges(n_f)
    start_sums(n_f)

    @pl.loop(0, n_f)
    def _(r):
        @pl.when(done_at(r) < n_f)
        def _():
            send_out(r)

    finish_rows(n_f)

    @pl.loop(0, n_f)
    def _(r):
        @pl.when(done_at(r) == n_f)
        def _():
            send_out(r)

    if n_s > 2:
        own_rows()

    def share_grad(q):
        g_copy(q, 0).wait_recv()
        h_copy(q, c).start()

    def take_grad(q):
        h_copy(q, sibling).wait_recv()
        place = lanes(q, cols)
        store_shifts(grads, place, grads[1, :, place])

    for block in x_peers:
        start = early_row(block, n_f)

        @pl.loop(1, last)
        def _(q):
            for h in range(2):
                wait_row(block * n_f + q, h)

        @pl.loop(0, n_f - 1)
        def _(q):
            share_grad(start + q)

        @pl.loop(0, n_f - 1)
        def _(q):
            take_grad(start + q)

        @pl.loop(0, 9)
        def _(k):
            gw_own[k] += rows_tap(rows, grads, k // 3, lax.rem(k, 3), start, n_f - 1)

    for block in x_peers:
        share_grad(late_row(block, n_f))
        take_grad(late_row(block, n_f))

    @pl.loop(0, n_f)
    def _(r):
        sum_copy(r).wait_send()

        @pl.when(r == p)
        def _():
            own_out.wait()

        @pl.when(r != p)
        def _():
            out_copy(r).wait_send()
            pltpu.make_async_remote_copy(
                src_ref=act.at[r, :, pl.ds(0, half_c)],
                dst_ref=out.at[pl.ds(pl.multiple_of(r * o, o), o), :],
                send_sem=out_send.at[r], recv_sem=out_recv.at[r],
                device_id={"filt": r}, device_id_type=MESH,
            ).wait_recv()

        for d in range(n_s - 1):
            g_copy(first + r, d).wait_send()

            @pl.when(crosses(r))
            def _():
                for h in range(2):
                    to_x(r, h, d).wait_send()

        @pl.when((r <= p) & (p < last))
        def _():
            for h in range(2):
                to_right(first + r, h).wait_send()

        @pl.when((r >= p) & (p > 0))
        def _():
            for h in range(2):
                to_left(first + r, h).wait_send()

    for block in x_peers:
        @pl.loop(0, n_f)
        def _(q):
            h_copy(block * n_f + q, c).wait_send()

        for h in range(2):
            @pl.when(p < last)
            def _():
                to_right(block * n_f, h).wait_send()

            @pl.when(p > 0)
            def _():
                to_left(block * n_f + last, h).wait_send()


def finish_kernel(n_f, n_s, rows, grads, gw_own, out_in, gw, gb, out, total, sem, out_sem):
    out_copy = pltpu.make_async_copy(out_in, out.at[0], out_sem)
    out_copy.start()

    late = [(n_f - 1, min(n_s, 2))] + [(block * n_f, 1) for block in range(2, n_s)]

    def gw_copy(k):
        return pltpu.make_async_copy(total.at[k], gw.at[k // 3, lax.rem(k, 3)], sem.at[k])

    @pl.loop(0, 9)
    def _(k):
        value = gw_own[k]
        for start, count in late:
            value = value + rows_tap(rows, grads, k // 3, lax.rem(k, 3), start, count)
        total[k] = value
        gw_copy(k).start()

    gb[...] = lax.dot_general(
        jnp.ones((8, grads.shape[2]), jnp.bfloat16), grads[1], NT, preferred_element_type=jnp.float32
    )[:1]

    @pl.loop(0, 9)
    def _(k):
        gw_copy(k).wait()

    out_copy.wait()


def on_device(image, weight, bias, cotangent):
    n_f, n_s, n_in = (lax.axis_size(name) for name in ("filt", "sp", "in"))
    row_count, o, cols = cotangent.shape
    depth = image.shape[2]
    total = n_f * n_s
    any_space = pl.BlockSpec(memory_space=pl.ANY)
    vmem = pl.BlockSpec(memory_space=pltpu.VMEM)
    hbm = pl.BlockSpec(memory_space=pltpu.HBM)
    dma = pltpu.SemaphoreType.DMA
    between = pl.pallas_call(
        functools.partial(gather_kernel, n_f, n_s),
        out_shape=(
            pltpu.VMEM((total + 2, cols, depth), jnp.bfloat16),
            pltpu.VMEM((3, o, total * cols), jnp.bfloat16),
            pltpu.VMEM((9, o, depth), jnp.float32),
            pltpu.VMEM((n_f * o, cols // n_in), jnp.bfloat16),
        ),
        in_specs=[hbm, hbm, hbm, hbm],
        out_specs=(vmem,) * 4,
        scratch_shapes=[
            pltpu.VMEM((3, 3, o, depth), jnp.bfloat16),
            pltpu.VMEM((1, o), jnp.float32),
            pltpu.VMEM((n_f, o, cols), jnp.bfloat16),
            pltpu.VMEM((n_f + 2, o, cols), jnp.float32),
            pltpu.VMEM((n_f, o, cols), jnp.float32),
            pltpu.VMEM((n_f, o, cols), jnp.bfloat16),
            dma((4,)),
            dma((2, total, 2)),
            dma((total, 2)),
            dma((n_s - 1, n_f, 2)),
            dma((n_f,)),
            dma((n_f,)),
            dma((n_s - 1, total)),
            dma((total,)),
            dma((total,)),
            dma((total,)),
            dma((n_f,)),
            dma((n_f,)),
        ],
        compiler_params=pltpu.CompilerParams(
            collective_id=0, has_side_effects=True, vmem_limit_bytes=24 * 1024 * 1024
        ),
        name="gather",
    )(*(
        pltpu.with_memory_space_constraint(x, pltpu.HBM)
        for x in (image, weight, bias.reshape(1, o), cotangent)
    ))
    grad_weight, grad_bias, output = pl.pallas_call(
        functools.partial(finish_kernel, n_f, n_s),
        out_shape=(
            jax.ShapeDtypeStruct((3, 3, o, depth), jnp.float32),
            jax.ShapeDtypeStruct((1, o), jnp.float32),
            jax.ShapeDtypeStruct((1, n_f * o, cols // n_in), jnp.bfloat16),
        ),
        in_specs=[vmem] * 4,
        out_specs=(any_space, vmem, any_space),
        scratch_shapes=[
            pltpu.VMEM((9, o, depth), jnp.float32),
            dma((9,)),
            dma(()),
        ],
        compiler_params=pltpu.CompilerParams(vmem_limit_bytes=20 * 1024 * 1024),
        name="finish",
    )(*between)
    return (output, grad_weight, grad_bias.reshape(o))


def solution(mesh):
    placed = (
        P(("groups", "sp", "filt"), None, "in"),
        P(None, None, "filt", None),
        P("filt"),
        P(("groups", "sp"), "filt", None),
    )
    return jax.shard_map(
        on_device,
        mesh=mesh,
        in_specs=placed,
        out_specs=(
            P(("groups", "sp", "filt"), None, "in"),
            P("groups", None, "filt", "in"),
            P(("groups", "filt")),
        ),
        check_vma=False,
    )
```

profile of v0, /device:TPU:1, one launch (start us, length us, event | category | flops | bytes accessed | tf_op | source)
XLA Modules:
  0.0 43.5 jit_solution(11111342838921641314)
XLA Ops:
  0.6 38.6 %gather.1 = (bf16[10,256,512]{2,1,0:T(8,128)(2,1)S(1)}, bf16[3,256,2048]{2,1,0:T(8,128)(2,1)S(1)}, f32[9,256,512]{2,1,0:T(8,128)S(1)}, bf16[1024,128]{1,0:T(8,128)(2,1)S(1)}) custom-call(bf16[1,256,512]{2,1,0:T(8,128)(2,1)} %image.1, bf16[3,3,256,1024]{3,2,1,0:T(8,128)(2,1)} %weight.1, f32[1,256]{1,0:T(1,128)} %bitcast.2, bf16[4,256,256]{2,1,0:T(8,128)(2,1)} %cotangent.1), custom_call_target="tpu_custom_call" | custom-call | tf_op jit(solution)/shard_map/gather/pallas_call | solution.py:443
  39.3 4.2 %finish.1 = (f32[3,3,256,512]{3,2,1,0:T(8,128)}, f32[1,256]{1,0:T(1,128)}, bf16[1,1024,128]{2,1,0:T(8,128)(2,1)}) custom-call(bf16[10,256,512]{2,1,0:T(8,128)(2,1)S(1)} %get-tuple-element.10.rows, bf16[3,256,2048]{2,1,0:T(8,128)(2,1)S(1)} %get-tuple-element.11.grads, f32[9,256,512]{2,1,0:T(8,128)S(1)} %get-tuple-element.12.gw_own, ...), custom_call_target="tpu_custom_call" | custom-call | tf_op jit(solution)/shard_map/finish/pallas_call | solution.py:481
where the time goes:
time: 43.9 us; the launch traced here: 43.5 us
  Pallas kernels  42.9 us (98%)
  between operations  0.64 us (1%)
    pallas_call x1, Pallas kernels, on_device(): pl.pallas_call(functools.partial(gather_kernel, n_f, n_s), out_shape=(plt...  38.6 us
    pallas_call x1, Pallas kernels, on_device(): pl.pallas_call(functools.partial(finish_kernel, n_f, n_s), out_shape=(jax...  4.24 us

commit v1 on v0

--- a/solution.py
+++ b/solution.py
@@ -50,7 +50,7 @@
     image, weight, bias_in, cotangent,
     rows, grads, gw_own, out,
     w, bias, cot, part, peer, act,
-    load_sem, row_send, row_recv, x_send, sum_send, sum_recv,
+    load_sem, ready_z, ready_x, row_send, row_recv, x_send, sum_send, sum_recv,
     g_send, g_recv, h_send, h_recv, out_send, out_recv,
 ):
     p, s, c = lax.axis_index("filt"), lax.axis_index("sp"), lax.axis_index("in")
@@ -75,12 +75,18 @@
     load_bias.start()
 
     barrier = pltpu.get_barrier_semaphore()
-    for d in range(1, n_f):
-        pl.semaphore_signal(barrier, 1, device_id={"filt": lax.rem(p + d, n_f)}, device_id_type=MESH)
+
+    @pl.when(p < last)
+    def _():
+        pl.semaphore_signal(barrier, 1, device_id={"filt": p + 1}, device_id_type=MESH)
+
     for peer_s in x_peers:
-        pl.semaphore_signal(barrier, 1, device_id={"sp": peer_s}, device_id_type=MESH)
+        @pl.when(peer_s > s)
+        def _():
+            pl.semaphore_signal(barrier, 1, device_id={"sp": peer_s}, device_id_type=MESH)
+
     pl.semaphore_signal(barrier, 1, device_id={"in": sibling}, device_id_type=MESH)
-    pl.semaphore_wait(barrier, n_f - 1 + n_s - 1 + 1)
+    pl.semaphore_wait(barrier, 1 + s + jnp.where(p > 0, 1, 0))
 
     piece = cols // 2
 
@@ -121,9 +127,45 @@
             for d in range(n_s - 1):
                 to_x(q, h, d).start()
 
+    def own_copy(h, way, where, send):
+        place = pl.ds(h * piece, piece)
+        return pltpu.make_async_remote_copy(
+            src_ref=image.at[0, place], dst_ref=rows.at[1 + first + p, place],
+            send_sem=send, recv_sem=row_recv.at[first + p, h],
+            device_id={way: where}, device_id_type=MESH,
+        )
+
+    def own_to_x(up):
+        for d in range(n_s - 1):
+            @pl.when((x_peers[d] > s) if up else (x_peers[d] < s))
+            def _():
+                for h in range(2):
+                    own_copy(h, "sp", x_peers[d], x_send.at[d, p, h]).start()
+
+    @pl.when(p > 0)
+    def _():
+        for h in range(2):
+            own_copy(h, "filt", p - 1, row_send.at[1, first + p, h]).start()
+        pl.semaphore_signal(ready_z, 1, device_id={"filt": p - 1}, device_id_type=MESH)
+
+    own_to_x(False)
+    for peer_s in x_peers:
+        @pl.when(peer_s < s)
+        def _():
+            pl.semaphore_signal(ready_x, 1, device_id={"sp": peer_s}, device_id_type=MESH)
+
+    @pl.when(p < last)
+    def _():
+        pl.semaphore_wait(ready_z, 1)
+        for h in range(2):
+            own_copy(h, "filt", p + 1, row_send.at[0, first + p, h]).start()
+
+    @pl.when(s < n_s - 1)
+    def _():
+        pl.semaphore_wait(ready_x, n_s - 1 - s)
+
+    own_to_x(True)
     load_row.wait()
-    for h in range(2):
-        pass_on(p, h, True, True)
 
     zero = jnp.zeros((cols, depth), rows.dtype)
     rows[0] = zero
@@ -458,6 +500,8 @@
             pltpu.VMEM((n_f, o, cols), jnp.float32),
             pltpu.VMEM((n_f, o, cols), jnp.bfloat16),
             dma((4,)),
+            pltpu.SemaphoreType.REGULAR,
+            pltpu.SemaphoreType.REGULAR,
             dma((2, total, 2)),
             dma((total, 2)),
             dma((n_s - 1, n_f, 2)),

time: 43.9 us -> 41.9 us (0.954)
  Pallas kernels: 42.9 us -> 40.5 us
    pallas_call x1, Pallas kernels: 38.6 us -> 36.2 us  [on_device(): pl.pallas_call(functools.partial(gather_kernel, n_f, n_s), out_shape=(plt...]
where the time goes in v1:
time: 41.9 us; the launch traced here: 41.1 us
  Pallas kernels  40.5 us (97%)
  between operations  0.64 us (2%)
    pallas_call x1, Pallas kernels, on_device(): pl.pallas_call(functools.partial(gather_kernel, n_f, n_s), out_shape=(plt...  36.2 us
    pallas_call x1, Pallas kernels, on_device(): pl.pallas_call(functools.partial(finish_kernel, n_f, n_s), out_shape=(jax...  4.24 us

profile of v1, /device:TPU:1, one launch (start us, length us, event | category | flops | bytes accessed | tf_op | source)
XLA Modules:
  0.0 41.1 jit_solution(2220460858694591378)
XLA Ops:
  0.6 36.2 %gather.1 = (bf16[10,256,512]{2,1,0:T(8,128)(2,1)S(1)}, bf16[3,256,2048]{2,1,0:T(8,128)(2,1)S(1)}, f32[9,256,512]{2,1,0:T(8,128)S(1)}, bf16[1024,128]{1,0:T(8,128)(2,1)S(1)}) custom-call(bf16[1,256,512]{2,1,0:T(8,128)(2,1)} %image.1, bf16[3,3,256,1024]{3,2,1,0:T(8,128)(2,1)} %weight.1, f32[1,256]{1,0:T(1,128)} %bitcast.2, bf16[4,256,256]{2,1,0:T(8,128)(2,1)} %cotangent.1), custom_call_target="tpu_custom_call" | custom-call | tf_op jit(solution)/shard_map/gather/pallas_call | solution.py:485
  36.9 4.2 %finish.1 = (f32[3,3,256,512]{3,2,1,0:T(8,128)}, f32[1,256]{1,0:T(1,128)}, bf16[1,1024,128]{2,1,0:T(8,128)(2,1)}) custom-call(bf16[10,256,512]{2,1,0:T(8,128)(2,1)S(1)} %get-tuple-element.10.rows, bf16[3,256,2048]{2,1,0:T(8,128)(2,1)S(1)} %get-tuple-element.11.grads, f32[9,256,512]{2,1,0:T(8,128)S(1)} %get-tuple-element.12.gw_own, ...), custom_call_target="tpu_custom_call" | custom-call | tf_op jit(solution)/shard_map/finish/pallas_call | solution.py:525

commit v2 on v1

--- a/solution.py
+++ b/solution.py
@@ -29,11 +29,18 @@
     grads[2, :, place] = shift_cols(wide, -1).astype(jnp.bfloat16)
 
 
-def rows_tap(rows, grads, a, b, start, count):
+def rows_tap(rows, grads, a, start, count):
     cols, depth = rows.shape[1], rows.shape[2]
+    o = grads.shape[1]
     window = rows[pl.ds(start + a, count)].reshape(count * cols, depth)
-    return jnp.dot(
-        grads[b, :, lanes(start, cols, count)], window, preferred_element_type=jnp.float32
+    left = grads[:, :, lanes(start, cols, count)].reshape(3 * o, count * cols)
+    return jnp.dot(left, window, preferred_element_type=jnp.float32).reshape(3, o, depth)
+
+
+def bias_tap(grads, cols, start, count):
+    ones = jnp.ones((8, count * cols), jnp.bfloat16)
+    return lax.dot_general(
+        ones, grads[1, :, lanes(start, cols, count)], NT, preferred_element_type=jnp.float32
     )
 
 
@@ -48,7 +55,7 @@
 def gather_kernel(
     n_f, n_s,
     image, weight, bias_in, cotangent,
-    rows, grads, gw_own, out,
+    rows, grads, gw_own, gb_own, out,
     w, bias, cot, part, peer, act,
     load_sem, ready_z, ready_x, row_send, row_recv, x_send, sum_send, sum_recv,
     g_send, g_recv, h_send, h_recv, out_send, out_recv,
@@ -109,8 +116,8 @@
     def wait_row(q, h):
         row_copy(q, h, "filt", p, row_send.at[0, 0, 0]).wait_recv()
 
-    def crosses(q):
-        return ((q > 0) & (q < last)) | (q == p)
+    def crosses(q, h):
+        return ((q > 0) & (q < last)) | (q == p) | (h == 0)
 
     def pass_on(q, h, right, left):
         if right:
@@ -122,7 +129,7 @@
             def _():
                 to_left(first + q, h).start()
 
-        @pl.when(crosses(q))
+        @pl.when(crosses(q, h))
         def _():
             for d in range(n_s - 1):
                 to_x(q, h, d).start()
@@ -184,8 +191,12 @@
         part[r + 1] += shift_cols(sums[:o], -1) + sums[o:2 * o] + shift_cols(sums[2 * o:], 1)
 
     def add_row(q):
+        sums = lax.dot_general(
+            w[...].reshape(9 * o, depth), rows[1 + first + q], NT, preferred_element_type=jnp.float32
+        )
         for a in range(3):
-            add_tap(first + q, a, q - a + 1)
+            left, middle, right = (sums[(3 * a + b) * o:(3 * a + b + 1) * o] for b in range(3))
+            part[q - a + 2] += shift_cols(left, -1) + middle + shift_cols(right, 1)
 
     def sum_copy(r):
         return pltpu.make_async_remote_copy(
@@ -265,22 +276,24 @@
         @pl.when(t == p + 1)
         def _():
             for block in x_peers:
-                for h in range(2):
-                    wait_row(block * n_f, h)
-
-                    @pl.when(p < last)
-                    def _():
-                        to_right(block * n_f, h).start()
+                wait_row(block * n_f, 1)
+
+                @pl.when(p < last)
+                def _():
+                    to_right(block * n_f, 1).start()
+
+                wait_row(block * n_f, 0)
 
         @pl.when(t == n_f - p)
         def _():
             for block in x_peers:
-                for h in range(2):
-                    wait_row(block * n_f + last, h)
-
-                    @pl.when(p > 0)
-                    def _():
-                        to_left(block * n_f + last, h).start()
+                wait_row(block * n_f + last, 1)
+
+                @pl.when(p > 0)
+                def _():
+                    to_left(block * n_f + last, 1).start()
+
+                wait_row(block * n_f + last, 0)
 
     def add_edges(t):
         @pl.when((t == p + 1) & (s < n_s - 1))
@@ -332,34 +345,31 @@
         start_sums(t)
         finish_rows(t - 1)
 
-    def own_rows():
-        @pl.loop(0, 9)
-        def _(k):
-            gw_own[k] = rows_tap(rows, grads, k // 3, lax.rem(k, 3), early_row(s, n_f), n_f - 1)
+    early = early_row(s, n_f)
+
+    def own_rows(a):
+        gw_own[3 * a:3 * a + 3] = rows_tap(rows, grads, a, early, n_f - 1)
+
+    def send_outs(when):
+        @pl.loop(0, n_f)
+        def _(r):
+            @pl.when(when(done_at(r)))
+            def _():
+                send_out(r)
 
     finish_rows(n_f - 1)
-    if n_s <= 2:
-        own_rows()
+    send_outs(lambda done: done < n_f)
     relay(n_f)
     add_edges(n_f)
     start_sums(n_f)
-
-    @pl.loop(0, n_f)
-    def _(r):
-        @pl.when(done_at(r) < n_f)
-        def _():
-            send_out(r)
-
+    covering = 2 if n_s <= 2 else 0
+    for a in range(covering):
+        own_rows(a)
     finish_rows(n_f)
-
-    @pl.loop(0, n_f)
-    def _(r):
-        @pl.when(done_at(r) == n_f)
-        def _():
-            send_out(r)
-
-    if n_s > 2:
-        own_rows()
+    send_outs(lambda done: done == n_f)
+    for a in range(covering, 3):
+        own_rows(a)
+    gb_own[...] = bias_tap(grads, cols, early, n_f - 1)
 
     def share_grad(q):
         g_copy(q, 0).wait_recv()
@@ -386,9 +396,10 @@
         def _(q):
             take_grad(start + q)
 
-        @pl.loop(0, 9)
-        def _(k):
-            gw_own[k] += rows_tap(rows, grads, k // 3, lax.rem(k, 3), start, n_f - 1)
+        for a in range(3):
+            gw_own[3 * a:3 * a + 3] += rows_tap(rows, grads, a, start, n_f - 1)
+
+        gb_own[...] += bias_tap(grads, cols, start, n_f - 1)
 
     for block in x_peers:
         share_grad(late_row(block, n_f))
@@ -415,9 +426,9 @@
         for d in range(n_s - 1):
             g_copy(first + r, d).wait_send()
 
-            @pl.when(crosses(r))
-            def _():
-                for h in range(2):
+            for h in range(2):
+                @pl.when(crosses(r, h))
+                def _():
                     to_x(r, h, d).wait_send()
 
         @pl.when((r <= p) & (p < last))
@@ -435,40 +446,39 @@
         def _(q):
             h_copy(block * n_f + q, c).wait_send()
 
-        for h in range(2):
-            @pl.when(p < last)
-            def _():
-                to_right(block * n_f, h).wait_send()
-
-            @pl.when(p > 0)
-            def _():
-                to_left(block * n_f + last, h).wait_send()
-
-
-def finish_kernel(n_f, n_s, rows, grads, gw_own, out_in, gw, gb, out, total, sem, out_sem):
+        @pl.when(p < last)
+        def _():
+            to_right(block * n_f, 1).wait_send()
+
+        @pl.when(p > 0)
+        def _():
+            to_left(block * n_f + last, 1).wait_send()
+
+
+def finish_kernel(n_f, n_s, rows, grads, gw_own, gb_own, out_in, gw, gb, out, total, sem, out_sem):
+    cols = rows.shape[1]
     out_copy = pltpu.make_async_copy(out_in, out.at[0], out_sem)
     out_copy.start()
 
     late = [(n_f - 1, min(n_s, 2))] + [(block * n_f, 1) for block in range(2, n_s)]
 
-    def gw_copy(k):
-        return pltpu.make_async_copy(total.at[k], gw.at[k // 3, lax.rem(k, 3)], sem.at[k])
-
-    @pl.loop(0, 9)
-    def _(k):
-        value = gw_own[k]
+    def gw_copy(a):
+        return pltpu.make_async_copy(total.at[a], gw.at[a], sem.at[a])
+
+    for a in range(3):
+        value = gw_own[3 * a:3 * a + 3]
         for start, count in late:
-            value = value + rows_tap(rows, grads, k // 3, lax.rem(k, 3), start, count)
-        total[k] = value
-        gw_copy(k).start()
-
-    gb[...] = lax.dot_general(
-        jnp.ones((8, grads.shape[2]), jnp.bfloat16), grads[1], NT, preferred_element_type=jnp.float32
-    )[:1]
-
-    @pl.loop(0, 9)
-    def _(k):
-        gw_copy(k).wait()
+            value = value + rows_tap(rows, grads, a, start, count)
+        total[a] = value
+        gw_copy(a).start()
+
+    bias = gb_own[...]
+    for start, count in late:
+        bias = bias + bias_tap(grads, cols, start, count)
+    gb[...] = bias[:1]
+
+    for a in range(3):
+        gw_copy(a).wait()
 
     out_copy.wait()
 
@@ -488,10 +498,11 @@
             pltpu.VMEM((total + 2, cols, depth), jnp.bfloat16),
             pltpu.VMEM((3, o, total * cols), jnp.bfloat16),
             pltpu.VMEM((9, o, depth), jnp.float32),
+            pltpu.VMEM((8, o), jnp.float32),
             pltpu.VMEM((n_f * o, cols // n_in), jnp.bfloat16),
         ),
         in_specs=[hbm, hbm, hbm, hbm],
-        out_specs=(vmem,) * 4,
+        out_specs=(vmem,) * 5,
         scratch_shapes=[
             pltpu.VMEM((3, 3, o, depth), jnp.bfloat16),
             pltpu.VMEM((1, o), jnp.float32),
@@ -529,11 +540,11 @@
             jax.ShapeDtypeStruct((1, o), jnp.float32),
             jax.ShapeDtypeStruct((1, n_f * o, cols // n_in), jnp.bfloat16),
         ),
-        in_specs=[vmem] * 4,
+        in_specs=[vmem] * 5,
         out_specs=(any_space, vmem, any_space),
         scratch_shapes=[
-            pltpu.VMEM((9, o, depth), jnp.float32),
-            dma((9,)),
+            pltpu.VMEM((3, 3, o, depth), jnp.float32),
+            dma((3,)),
             dma(()),
         ],
         compiler_params=pltpu.CompilerParams(vmem_limit_bytes=20 * 1024 * 1024),

time: 41.9 us -> 39.3 us (0.938)
  Pallas kernels: 40.5 us -> 38 us
    pallas_call x1, Pallas kernels: 36.2 us -> 34.5 us  [on_device(): pl.pallas_call(functools.partial(gather_kernel, n_f, n_s), out_shape=(plt...]
    pallas_call x1, Pallas kernels: 4.24 us -> 3.44 us  [on_device(): pl.pallas_call(functools.partial(finish_kernel, n_f, n_s), out_shape=(jax...]
where the time goes in v2:
time: 39.3 us; the launch traced here: 38.6 us
  Pallas kernels  38 us (97%)
  between operations  0.64 us (2%)
    pallas_call x1, Pallas kernels, on_device(): pl.pallas_call(functools.partial(gather_kernel, n_f, n_s), out_shape=(plt...  34.5 us
    pallas_call x1, Pallas kernels, on_device(): pl.pallas_call(functools.partial(finish_kernel, n_f, n_s), out_shape=(jax...  3.44 us

profile of v2, /device:TPU:1, one launch (start us, length us, event | category | flops | bytes accessed | tf_op | source)
XLA Modules:
  0.0 38.6 jit_solution(14039333207367280465)
XLA Ops:
  0.6 34.5 %gather.1 = (bf16[10,256,512]{2,1,0:T(8,128)(2,1)S(1)}, bf16[3,256,2048]{2,1,0:T(8,128)(2,1)S(1)}, f32[9,256,512]{2,1,0:T(8,128)S(1)}, f32[8,256]{1,0:T(8,128)S(1)}, bf16[1024,128]{1,0:T(8,128)(2,1)S(1)}) custom-call(bf16[1,256,512]{2,1,0:T(8,128)(2,1)} %image.1, bf16[3,3,256,1024]{3,2,1,0:T(8,128)(2,1)} %weight.1, f32[1,256]{1,0:T(1,128)} %bitcast.2, ...), custom_call_target="tpu_custom_call" | custom-call | tf_op jit(solution)/shard_map/gather/pallas_call | solution.py:495
  35.2 3.4 %finish.1 = (f32[3,3,256,512]{3,2,1,0:T(8,128)}, f32[1,256]{1,0:T(1,128)}, bf16[1,1024,128]{2,1,0:T(8,128)(2,1)}) custom-call(bf16[10,256,512]{2,1,0:T(8,128)(2,1)S(1)} %get-tuple-element.11.rows, bf16[3,256,2048]{2,1,0:T(8,128)(2,1)S(1)} %get-tuple-element.12.grads, f32[9,256,512]{2,1,0:T(8,128)S(1)} %get-tuple-element.13.gw_own, ...), custom_call_target="tpu_custom_call" | custom-call | tf_op jit(solution)/shard_map/finish/pallas_call | solution.py:536

commit v3 on v2

--- a/solution.py
+++ b/solution.py
@@ -58,7 +58,7 @@
     rows, grads, gw_own, gb_own, out,
     w, bias, cot, part, peer, act,
     load_sem, ready_z, ready_x, row_send, row_recv, x_send, sum_send, sum_recv,
-    g_send, g_recv, h_send, h_recv, out_send, out_recv,
+    g_send, g_recv, h_send, h_recv, out_send, out_recv, cot_send, cot_recv,
 ):
     p, s, c = lax.axis_index("filt"), lax.axis_index("sp"), lax.axis_index("in")
     sibling = 1 - c
@@ -69,12 +69,21 @@
     first = s * n_f
     last = n_f - 1
     x_peers = [lax.rem(s + d, n_s) for d in range(1, n_s)]
+    pair = n_s == 2
+    other = 1 - s
+    low = p < n_f // 2
+    dist = jnp.where(low, p, last - p)
+    early = (low & (s == 0)) | ((p >= n_f // 2) & (s > 0))
+    late = (low & (s > 0)) | ((p >= n_f // 2) & (s == 0))
+    bound = jnp.where(s == 0, n_f, -1)
+    own_bound = jnp.where(s == 0, last, 0)
+    bound_at = jnp.maximum(last - dist, jnp.maximum(dist + 1, 2))
 
     load_row = pltpu.make_async_copy(image.at[0], rows.at[1 + first + p], load_sem.at[0])
     load_w = pltpu.make_async_copy(
         weight.at[:, :, :, pl.ds(pl.multiple_of(c * depth, depth), depth)], w, load_sem.at[1]
     )
-    load_cot = pltpu.make_async_copy(cotangent, cot, load_sem.at[2])
+    load_cot = pltpu.make_async_copy(cotangent, cot.at[pl.ds(1, n_f)], load_sem.at[2])
     load_bias = pltpu.make_async_copy(bias_in, bias, load_sem.at[3])
     load_row.start()
     load_w.start()
@@ -200,7 +209,8 @@
 
     def sum_copy(r):
         return pltpu.make_async_remote_copy(
-            src_ref=part.at[r + 1], dst_ref=peer.at[r], send_sem=sum_send.at[r], recv_sem=sum_recv.at[r],
+            src_ref=part.at[r + 1], dst_ref=peer.at[r + 1],
+            send_sem=sum_send.at[r + 1], recv_sem=sum_recv.at[r + 1],
             device_id={"in": sibling}, device_id_type=MESH,
         )
 
@@ -237,6 +247,24 @@
             device_id={"in": sibling}, device_id_type=MESH,
         )
 
+    def half(place, core):
+        return place.at[pl.ds(pl.multiple_of(core * half_o, half_o), half_o)]
+
+    def cot_copy():
+        return pltpu.make_async_remote_copy(
+            src_ref=half(cotangent.at[own_bound], c),
+            dst_ref=half(cot.at[jnp.where(s == 0, 0, n_f + 1)], c),
+            send_sem=cot_send.at[0], recv_sem=cot_recv.at[0],
+            device_id={"sp": other}, device_id_type=MESH,
+        )
+
+    def cot_share(core):
+        place = half(cot.at[bound + 1], core)
+        return pltpu.make_async_remote_copy(
+            src_ref=place, dst_ref=place, send_sem=cot_send.at[1], recv_sem=cot_recv.at[1],
+            device_id={"in": sibling}, device_id_type=MESH,
+        )
+
     def done_at(r):
         low = jnp.where(s == 0, jnp.maximum(p, 1), jnp.maximum(p, n_f - p))
         high = jnp.where(
@@ -244,20 +272,34 @@
         )
         return jnp.where(r == 0, low, jnp.where(r == last, high, jnp.abs(r - p) + 1))
 
-    def finish(r):
+    def sends_grad(r):
+        return early | (r != own_bound) if pair else r >= 0
+
+    def activate(r):
         sum_copy(r).wait_recv()
         bias_all = jnp.broadcast_to(bias[...], (cols, o)).T
-        shifted = part[r + 1] + peer[r] + bias_all
+        shifted = part[r + 1] + peer[r + 1] + bias_all
         sig = jax.nn.sigmoid(shifted)
         slope = sig * (1.0 + shifted * (1.0 - sig))
-        grad = (cot[r].astype(jnp.float32) * slope).astype(jnp.bfloat16)
-        place = lanes(first + r, cols)
-        grads[1, :, place] = grad
-        act[r] = (shifted * sig).astype(jnp.bfloat16)
-        for d in range(n_s - 1):
-            g_copy(first + r, d).start()
-
-        store_shifts(grads, place, grad)
+        grad = (cot[r + 1].astype(jnp.float32) * slope).astype(jnp.bfloat16)
+        grads[1, :, lanes(first + r, cols)] = grad
+        return grad, (shifted * sig).astype(jnp.bfloat16)
+
+    def finish(r):
+        grad, value = activate(r)
+        act[r] = value
+
+        @pl.when(sends_grad(r))
+        def _():
+            for d in range(n_s - 1):
+                g_copy(first + r, d).start()
+
+        send_out(r)
+        store_shifts(grads, lanes(first + r, cols), grad)
+
+    def finish_bound():
+        grad, _ = activate(bound)
+        store_shifts(grads, lanes(first + bound, cols), grad)
 
     def send_out(r):
         @pl.when(r == p)
@@ -296,6 +338,27 @@
                 wait_row(block * n_f + last, 0)
 
     def add_edges(t):
+        if pair:
+            tap = jnp.where(s == 0, 2, 0)
+            edge = jnp.where(s == 0, first + n_f, first - 1)
+            after = jnp.where(s == 0, first + n_f + 1, first - 2)
+
+            @pl.when(t == jnp.where(early, dist + 1, n_f - dist))
+            def _():
+                add_tap(edge, tap, own_bound)
+
+            @pl.when(early & (t == dist + 1))
+            def _():
+                add_tap(edge, 1, bound)
+
+            @pl.when(early & (t == jnp.maximum(dist + 1, 2)))
+            def _():
+                for h in range(2):
+                    wait_row(after, h)
+                add_tap(after, tap, bound)
+
+            return
+
         @pl.when((t == p + 1) & (s < n_s - 1))
         def _():
             add_tap(first + n_f, 2, last)
@@ -311,6 +374,11 @@
             def _():
                 sum_copy(r).start()
 
+        if pair:
+            @pl.when(early & (t == bound_at))
+            def _():
+                sum_copy(bound).start()
+
     def finish_rows(t):
         @pl.loop(0, n_f)
         def _(r):
@@ -343,33 +411,24 @@
 
         add_edges(t)
         start_sums(t)
-        finish_rows(t - 1)
-
-    early = early_row(s, n_f)
+
+        if pair:
+            @pl.when(late & (t == n_f - 2))
+            def _():
+                cot_copy().start()
+
+        finish_rows(t)
+
+    own_start = early_row(s, n_f)
 
     def own_rows(a):
-        gw_own[3 * a:3 * a + 3] = rows_tap(rows, grads, a, early, n_f - 1)
-
-    def send_outs(when):
-        @pl.loop(0, n_f)
-        def _(r):
-            @pl.when(when(done_at(r)))
-            def _():
-                send_out(r)
-
-    finish_rows(n_f - 1)
-    send_outs(lambda done: done < n_f)
-    relay(n_f)
-    add_edges(n_f)
-    start_sums(n_f)
-    covering = 2 if n_s <= 2 else 0
-    for a in range(covering):
-        own_rows(a)
-    finish_rows(n_f)
-    send_outs(lambda done: done == n_f)
-    for a in range(covering, 3):
-        own_rows(a)
-    gb_own[...] = bias_tap(grads, cols, early, n_f - 1)
+        gw_own[3 * a:3 * a + 3] = rows_tap(rows, grads, a, own_start, n_f - 1)
+
+    def add_rows(a, start, count):
+        gw_own[3 * a:3 * a + 3] += rows_tap(rows, grads, a, start, count)
+
+    def add_bias(start, count):
+        gb_own[...] += bias_tap(grads, cols, start, count)
 
     def share_grad(q):
         g_copy(q, 0).wait_recv()
@@ -380,30 +439,122 @@
         place = lanes(q, cols)
         store_shifts(grads, place, grads[1, :, place])
 
-    for block in x_peers:
-        start = early_row(block, n_f)
-
-        @pl.loop(1, last)
-        def _(q):
+    def tail_of_pair():
+        near = n_f // 2
+
+        def place(k):
+            return other * n_f + jnp.where(low, k, last - k)
+
+        @pl.when(early)
+        def _():
+            cot_copy().wait_recv()
+            cot_share(c).start()
+
+        @pl.when(late)
+        def _():
+            relay(n_f)
+            add_edges(n_f)
+            start_sums(n_f)
+
+        own_rows(0)
+        own_rows(1)
+
+        @pl.when(early)
+        def _():
+            cot_share(sibling).wait_recv()
+            finish_bound()
+
+        finish_rows(n_f)
+
+        @pl.when(late)
+        def _():
+            share_grad(place(0))
+
+        @pl.loop(1, near)
+        def _(k):
+            share_grad(place(k))
+
+        own_rows(2)
+        gb_own[...] = bias_tap(grads, cols, own_start, n_f - 1)
+
+        @pl.when(late)
+        def _():
             for h in range(2):
-                wait_row(block * n_f + q, h)
-
-        @pl.loop(0, n_f - 1)
-        def _(q):
-            share_grad(start + q)
-
-        @pl.loop(0, n_f - 1)
-        def _(q):
-            take_grad(start + q)
-
+                wait_row(place(1), h)
+            take_grad(place(0))
+
+        @pl.when(early)
+        def _():
+            relay(n_f)
+
+        @pl.loop(2, last)
+        def _(k):
+            for h in range(2):
+                wait_row(place(k), h)
+
+        @pl.loop(1, near)
+        def _(k):
+            take_grad(place(k))
+
+        some = jnp.where(
+            early, jnp.where(low, last, n_f - near + 1), jnp.where(low, 0, 2 * n_f - near)
+        )
+        one = jnp.where(
+            early, jnp.where(low, n_f + near - 1, n_f - near), jnp.where(low, n_f, last)
+        )
         for a in range(3):
-            gw_own[3 * a:3 * a + 3] += rows_tap(rows, grads, a, start, n_f - 1)
-
-        gb_own[...] += bias_tap(grads, cols, start, n_f - 1)
-
-    for block in x_peers:
-        share_grad(late_row(block, n_f))
-        take_grad(late_row(block, n_f))
+            add_rows(a, some, near)
+        for a in range(3):
+            add_rows(a, one, 1)
+        add_bias(some, near)
+        add_bias(one, 1)
+
+        @pl.loop(near, n_f)
+        def _(k):
+            share_grad(place(k))
+
+        @pl.loop(near, n_f)
+        def _(k):
+            take_grad(place(k))
+
+    def tail_of_many():
+        relay(n_f)
+        add_edges(n_f)
+        start_sums(n_f)
+        finish_rows(n_f)
+        for a in range(3):
+            own_rows(a)
+        gb_own[...] = bias_tap(grads, cols, own_start, n_f - 1)
+
+        for block in x_peers:
+            start = early_row(block, n_f)
+
+            @pl.loop(1, last)
+            def _(q):
+                for h in range(2):
+                    wait_row(block * n_f + q, h)
+
+            @pl.loop(0, n_f - 1)
+            def _(q):
+                share_grad(start + q)
+
+            @pl.loop(0, n_f - 1)
+            def _(q):
+                take_grad(start + q)
+
+            for a in range(3):
+                add_rows(a, start, n_f - 1)
+
+            add_bias(start, n_f - 1)
+
+        for block in x_peers:
+            share_grad(late_row(block, n_f))
+            take_grad(late_row(block, n_f))
+
+    if pair:
+        tail_of_pair()
+    else:
+        tail_of_many()
 
     @pl.loop(0, n_f)
     def _(r):
@@ -424,7 +575,9 @@
             ).wait_recv()
 
         for d in range(n_s - 1):
-            g_copy(first + r, d).wait_send()
+            @pl.when(sends_grad(r))
+            def _():
+                g_copy(first + r, d).wait_send()
 
             for h in range(2):
                 @pl.when(crosses(r, h))
@@ -444,7 +597,12 @@
     for block in x_peers:
         @pl.loop(0, n_f)
         def _(q):
-            h_copy(block * n_f + q, c).wait_send()
+            if pair:
+                @pl.when(late | (q != jnp.where(low, 0, last)))
+                def _():
+                    h_copy(block * n_f + q, c).wait_send()
+            else:
+                h_copy(block * n_f + q, c).wait_send()
 
         @pl.when(p < last)
         def _():
@@ -453,6 +611,16 @@
         @pl.when(p > 0)
         def _():
             to_left(block * n_f + last, 1).wait_send()
+
+    if pair:
+        @pl.when(early)
+        def _():
+            sum_copy(bound).wait_send()
+            cot_share(c).wait_send()
+
+        @pl.when(late)
+        def _():
+            cot_copy().wait_send()
 
 
 def finish_kernel(n_f, n_s, rows, grads, gw_own, gb_own, out_in, gw, gb, out, total, sem, out_sem):
@@ -460,7 +628,12 @@
     out_copy = pltpu.make_async_copy(out_in, out.at[0], out_sem)
     out_copy.start()
 
-    late = [(n_f - 1, min(n_s, 2))] + [(block * n_f, 1) for block in range(2, n_s)]
+    if n_s == 2:
+        p, s = lax.axis_index("filt"), lax.axis_index("sp")
+        near = n_f // 2
+        late = [((1 - s) * n_f + jnp.where(p < near, near, 0), n_f - near)]
+    else:
+        late = [(n_f - 1, 2)] + [(block * n_f, 1) for block in range(2, n_s)]
 
     def gw_copy(a):
         return pltpu.make_async_copy(total.at[a], gw.at[a], sem.at[a])
@@ -506,9 +679,9 @@
         scratch_shapes=[
             pltpu.VMEM((3, 3, o, depth), jnp.bfloat16),
             pltpu.VMEM((1, o), jnp.float32),
-            pltpu.VMEM((n_f, o, cols), jnp.bfloat16),
+            pltpu.VMEM((n_f + 2, o, cols), jnp.bfloat16),
             pltpu.VMEM((n_f + 2, o, cols), jnp.float32),
-            pltpu.VMEM((n_f, o, cols), jnp.float32),
+            pltpu.VMEM((n_f + 2, o, cols), jnp.float32),
             pltpu.VMEM((n_f, o, cols), jnp.bfloat16),
             dma((4,)),
             pltpu.SemaphoreType.REGULAR,
@@ -516,14 +689,16 @@
             dma((2, total, 2)),
             dma((total, 2)),
             dma((n_s - 1, n_f, 2)),
-            dma((n_f,)),
-            dma((n_f,)),
+            dma((n_f + 2,)),
+            dma((n_f + 2,)),
             dma((n_s - 1, total)),
             dma((total,)),
             dma((total,)),
             dma((total,)),
             dma((n_f,)),
             dma((n_f,)),
+            dma((2,)),
+            dma((2,)),
         ],
         compiler_params=pltpu.CompilerParams(
             collective_id=0, has_side_effects=True, vmem_limit_bytes=24 * 1024 * 1024

time: 39.3 us -> 39.9 us (1.015)
  Pallas kernels: 38 us -> 38.8 us
    pallas_call x1, Pallas kernels: 34.5 us -> 35.4 us  [on_device(): pl.pallas_call(functools.partial(gather_kernel, n_f, n_s), out_shape=(plt...]
where the time goes in v3:
time: 39.9 us; the launch traced here: 39.4 us
  Pallas kernels  38.8 us (97%)
  between operations  0.64 us (2%)
    pallas_call x1, Pallas kernels, on_device(): pl.pallas_call(functools.partial(gather_kernel, n_f, n_s), out_shape=(plt...  35.4 us
    pallas_call x1, Pallas kernels, on_device(): pl.pallas_call(functools.partial(finish_kernel, n_f, n_s), out_shape=(jax...  3.36 us

profile of v3, /device:TPU:1, one launch (start us, length us, event | category | flops | bytes accessed | tf_op | source)
XLA Modules:
  0.0 39.4 jit_solution(4978762020083815791)
XLA Ops:
  0.6 35.4 %gather.1 = (bf16[10,256,512]{2,1,0:T(8,128)(2,1)S(1)}, bf16[3,256,2048]{2,1,0:T(8,128)(2,1)S(1)}, f32[9,256,512]{2,1,0:T(8,128)S(1)}, f32[8,256]{1,0:T(8,128)S(1)}, bf16[1024,128]{1,0:T(8,128)(2,1)S(1)}) custom-call(bf16[1,256,512]{2,1,0:T(8,128)(2,1)} %image.1, bf16[3,3,256,1024]{3,2,1,0:T(8,128)(2,1)} %weight.1, f32[1,256]{1,0:T(1,128)} %bitcast.2, ...), custom_call_target="tpu_custom_call" | custom-call | tf_op jit(solution)/shard_map/gather/pallas_call | solution.py:668
  36.1 3.4 %finish.1 = (f32[3,3,256,512]{3,2,1,0:T(8,128)}, f32[1,256]{1,0:T(1,128)}, bf16[1,1024,128]{2,1,0:T(8,128)(2,1)}) custom-call(bf16[10,256,512]{2,1,0:T(8,128)(2,1)S(1)} %get-tuple-element.11.rows, bf16[3,256,2048]{2,1,0:T(8,128)(2,1)S(1)} %get-tuple-element.12.grads, f32[9,256,512]{2,1,0:T(8,128)S(1)} %get-tuple-element.13.gw_own, ...), custom_call_target="tpu_custom_call" | custom-call | tf_op jit(solution)/shard_map/finish/pallas_call | solution.py:711

commit v4 on v3

--- a/solution.py
+++ b/solution.py
@@ -78,6 +78,17 @@
     bound = jnp.where(s == 0, n_f, -1)
     own_bound = jnp.where(s == 0, last, 0)
     bound_at = jnp.maximum(last - dist, jnp.maximum(dist + 1, 2))
+    near = n_f // 2
+
+    def down_row(block):
+        return jnp.where(block == 0, last - 1, last)
+
+    def up_row(block):
+        return jnp.where(block == 0, 0, 1)
+
+    def relayed(q, block):
+        down, up = down_row(block), up_row(block)
+        return ((q == down) & (p < down)) | ((q == up) & (p > up))
 
     load_row = pltpu.make_async_copy(image.at[0], rows.at[1 + first + p], load_sem.at[0])
     load_w = pltpu.make_async_copy(
@@ -126,6 +137,8 @@
         row_copy(q, h, "filt", p, row_send.at[0, 0, 0]).wait_recv()
 
     def crosses(q, h):
+        if pair:
+            return jnp.logical_not(relayed(q, s))
         return ((q > 0) & (q < last)) | (q == p) | (h == 0)
 
     def pass_on(q, h, right, left):
@@ -192,6 +205,13 @@
         part[r] = jnp.zeros((o, cols), jnp.float32)
 
     load_w.wait()
+
+    if pair:
+        @pl.loop(0, 9)
+        def _(k):
+            gw_own[k] = jnp.zeros((o, depth), jnp.float32)
+
+        gb_own[...] = jnp.zeros(gb_own.shape, jnp.float32)
 
     def add_tap(q, a, r):
         sums = lax.dot_general(
@@ -314,7 +334,39 @@
     load_cot.wait()
     load_bias.wait()
 
+    def relay_pair(t):
+        down, up = down_row(other), up_row(other)
+
+        @pl.when((p <= down) & (t == jnp.where(p == down, 1, n_f - p)))
+        def _():
+            for h in range(2):
+                wait_row(other * n_f + down, h)
+
+                @pl.when(p > 0)
+                def _():
+                    to_left(other * n_f + down, h).start()
+
+        @pl.when((p >= up) & (t == jnp.where(p == up, 1, p + 1)))
+        def _():
+            for h in range(2):
+                wait_row(other * n_f + up, h)
+
+                @pl.when(p < last)
+                def _():
+                    to_right(other * n_f + up, h).start()
+
+    def arrive(q):
+        down, up = down_row(other), up_row(other)
+
+        @pl.when(jnp.logical_not(((q == down) & (p <= down)) | ((q == up) & (p >= up))))
+        def _():
+            for h in range(2):
+                wait_row(other * n_f + q, h)
+
     def relay(t):
+        if pair:
+            return relay_pair(t)
+
         @pl.when(t == p + 1)
         def _():
             for block in x_peers:
@@ -345,6 +397,7 @@
 
             @pl.when(t == jnp.where(early, dist + 1, n_f - dist))
             def _():
+                arrive(edge - other * n_f)
                 add_tap(edge, tap, own_bound)
 
             @pl.when(early & (t == dist + 1))
@@ -353,8 +406,7 @@
 
             @pl.when(early & (t == jnp.maximum(dist + 1, 2)))
             def _():
-                for h in range(2):
-                    wait_row(after, h)
+                arrive(after - other * n_f)
                 add_tap(after, tap, bound)
 
             return
@@ -386,39 +438,6 @@
             def _():
                 finish(r)
 
-    @pl.loop(1, n_f)
-    def _(t):
-        for h in range(2):
-            @pl.when(p - t >= 0)
-            def _():
-                wait_row(first + p - t, h)
-                pass_on(p - t, h, True, False)
-
-            @pl.when(p + t < n_f)
-            def _():
-                wait_row(first + p + t, h)
-                pass_on(p + t, h, False, True)
-
-        relay(t)
-
-        @pl.when(p - t >= 0)
-        def _():
-            add_row(p - t)
-
-        @pl.when(p + t < n_f)
-        def _():
-            add_row(p + t)
-
-        add_edges(t)
-        start_sums(t)
-
-        if pair:
-            @pl.when(late & (t == n_f - 2))
-            def _():
-                cot_copy().start()
-
-        finish_rows(t)
-
     own_start = early_row(s, n_f)
 
     def own_rows(a):
@@ -439,9 +458,21 @@
         place = lanes(q, cols)
         store_shifts(grads, place, grads[1, :, place])
 
+    def add_all(start, count):
+        for a in range(3):
+            add_rows(a, start, count)
+        add_bias(start, count)
+
+    def near_rows():
+        @pl.when(early)
+        def _():
+            add_all(first + jnp.where(low, 0, n_f - near), near)
+
+        @pl.when(late)
+        def _():
+            add_all(first + jnp.where(low, 1, n_f - near), near - 1)
+
     def tail_of_pair():
-        near = n_f // 2
-
         def place(k):
             return other * n_f + jnp.where(low, k, last - k)
 
@@ -452,70 +483,53 @@
 
         @pl.when(late)
         def _():
-            relay(n_f)
             add_edges(n_f)
             start_sums(n_f)
 
-        own_rows(0)
-        own_rows(1)
+        add_all(first + jnp.where(low, near, 0), n_f - near)
 
         @pl.when(early)
         def _():
+            share_grad(place(1))
             cot_share(sibling).wait_recv()
             finish_bound()
 
-        finish_rows(n_f)
+            @pl.loop(2, last)
+            def _(k):
+                arrive(place(k) - other * n_f)
 
         @pl.when(late)
         def _():
+            finish_rows(n_f)
             share_grad(place(0))
-
-        @pl.loop(1, near)
+            share_grad(place(1))
+            add_all(first + own_bound, 1)
+
+            @pl.loop(0, last - 1)
+            def _(k):
+                arrive(place(k) - other * n_f)
+
+            take_grad(place(0))
+
+        @pl.loop(2, near)
         def _(k):
             share_grad(place(k))
-
-        own_rows(2)
-        gb_own[...] = bias_tap(grads, cols, own_start, n_f - 1)
-
-        @pl.when(late)
-        def _():
-            for h in range(2):
-                wait_row(place(1), h)
-            take_grad(place(0))
-
-        @pl.when(early)
-        def _():
-            relay(n_f)
-
-        @pl.loop(2, last)
-        def _(k):
-            for h in range(2):
-                wait_row(place(k), h)
 
         @pl.loop(1, near)
         def _(k):
             take_grad(place(k))
 
-        some = jnp.where(
-            early, jnp.where(low, last, n_f - near + 1), jnp.where(low, 0, 2 * n_f - near)
-        )
-        one = jnp.where(
-            early, jnp.where(low, n_f + near - 1, n_f - near), jnp.where(low, n_f, last)
-        )
-        for a in range(3):
-            add_rows(a, some, near)
-        for a in range(3):
-            add_rows(a, one, 1)
-        add_bias(some, near)
-        add_bias(one, 1)
+        relay(n_f)
+        add_all(other * n_f + jnp.where(low, 0, n_f - near), near)
 
         @pl.loop(near, n_f)
         def _(k):
             share_grad(place(k))
-
-        @pl.loop(near, n_f)
-        def _(k):
             take_grad(place(k))
+
+            @pl.when(k < last)
+            def _():
+                add_all(place(k), 1)
 
     def tail_of_many():
         relay(n_f)
@@ -551,6 +565,44 @@
             share_grad(late_row(block, n_f))
             take_grad(late_row(block, n_f))
 
+    @pl.loop(1, n_f)
+    def _(t):
+        for h in range(2):
+            @pl.when(p - t >= 0)
+            def _():
+                wait_row(first + p - t, h)
+                pass_on(p - t, h, True, False)
+
+            @pl.when(p + t < n_f)
+            def _():
+                wait_row(first + p + t, h)
+                pass_on(p + t, h, False, True)
+
+        relay(t)
+
+        @pl.when(p - t >= 0)
+        def _():
+            add_row(p - t)
+
+        @pl.when(p + t < n_f)
+        def _():
+            add_row(p + t)
+
+        add_edges(t)
+        start_sums(t)
+
+        if pair:
+            @pl.when(late & (t == n_f - 2))
+            def _():
+                cot_copy().start()
+
+        finish_rows(t)
+
+        if pair:
+            @pl.when(t == n_f - 2)
+            def _():
+                near_rows()
+
     if pair:
         tail_of_pair()
     else:
@@ -593,6 +645,17 @@
         def _():
             for h in range(2):
                 to_left(first + r, h).wait_send()
+
+    if pair:
+        @pl.when((p <= down_row(other)) & (p > 0))
+        def _():
+            for h in range(2):
+                to_left(other * n_f + down_row(other), h).wait_send()
+
+        @pl.when((p >= up_row(other)) & (p < last))
+        def _():
+            for h in range(2):
+                to_right(other * n_f + up_row(other), h).wait_send()
 
     for block in x_peers:
         @pl.loop(0, n_f)
@@ -604,13 +667,14 @@
             else:
                 h_copy(block * n_f + q, c).wait_send()
 
-        @pl.when(p < last)
-        def _():
-            to_right(block * n_f, 1).wait_send()
-
-        @pl.when(p > 0)
-        def _():
-            to_left(block * n_f + last, 1).wait_send()
+        if not pair:
+            @pl.when(p < last)
+            def _():
+                to_right(block * n_f, 1).wait_send()
+
+            @pl.when(p > 0)
+            def _():
+                to_left(block * n_f + last, 1).wait_send()
 
     if pair:
         @pl.when(early)
@@ -630,28 +694,28 @@
 
     if n_s == 2:
         p, s = lax.axis_index("filt"), lax.axis_index("sp")
-        near = n_f // 2
-        late = [((1 - s) * n_f + jnp.where(p < near, near, 0), n_f - near)]
+        late = [((1 - s) * n_f + jnp.where(p < n_f // 2, n_f - 1, 0), 1)]
     else:
         late = [(n_f - 1, 2)] + [(block * n_f, 1) for block in range(2, n_s)]
 
-    def gw_copy(a):
-        return pltpu.make_async_copy(total.at[a], gw.at[a], sem.at[a])
+    def gw_copy(k):
+        return pltpu.make_async_copy(total.at[k], gw.at[k // 3, k % 3], sem.at[k])
+
+    bias = gb_own[...]
+    for start, count in late:
+        bias = bias + bias_tap(grads, cols, start, count)
+    gb[...] = bias[:1]
 
     for a in range(3):
         value = gw_own[3 * a:3 * a + 3]
         for start, count in late:
             value = value + rows_tap(rows, grads, a, start, count)
-        total[a] = value
-        gw_copy(a).start()
-
-    bias = gb_own[...]
-    for start, count in late:
-        bias = bias + bias_tap(grads, cols, start, count)
-    gb[...] = bias[:1]
-
-    for a in range(3):
-        gw_copy(a).wait()
+        for b in range(3):
+            total[3 * a + b] = value[b]
+            gw_copy(3 * a + b).start()
+
+    for k in range(9):
+        gw_copy(k).wait()
 
     out_copy.wait()
 
@@ -718,8 +782,8 @@
         in_specs=[vmem] * 5,
         out_specs=(any_space, vmem, any_space),
         scratch_shapes=[
-            pltpu.VMEM((3, 3, o, depth), jnp.float32),
-            dma((3,)),
+            pltpu.VMEM((9, o, depth), jnp.float32),
+            dma((9,)),
             dma(()),
         ],
         compiler_params=pltpu.CompilerParams(vmem_limit_bytes=20 * 1024 * 1024),

time: 39.9 us -> 43.3 us (1.085)
  Pallas kernels: 38.8 us -> 42.3 us
    pallas_call x1, Pallas kernels: 35.4 us -> 39.2 us  [on_device(): pl.pallas_call(functools.partial(gather_kernel, n_f, n_s), out_shape=(plt...]
where the time goes in v4:
time: 43.3 us; the launch traced here: 43.1 us
  Pallas kernels  42.3 us (98%)
  between operations  0.8 us (2%)
    pallas_call x1, Pallas kernels, on_device(): pl.pallas_call(functools.partial(gather_kernel, n_f, n_s), out_shape=(plt...  39.2 us
    pallas_call x1, Pallas kernels, on_device(): pl.pallas_call(functools.partial(finish_kernel, n_f, n_s), out_shape=(jax...  3.16 us

profile of v4, /device:TPU:1, one launch (start us, length us, event | category | flops | bytes accessed | tf_op | source)
XLA Modules:
  0.0 43.1 jit_solution(11659344634027364481)
XLA Ops:
  0.6 39.2 %gather.1 = (bf16[10,256,512]{2,1,0:T(8,128)(2,1)S(1)}, bf16[3,256,2048]{2,1,0:T(8,128)(2,1)S(1)}, f32[9,256,512]{2,1,0:T(8,128)S(1)}, f32[8,256]{1,0:T(8,128)S(1)}, bf16[1024,128]{1,0:T(8,128)(2,1)S(1)}) custom-call(bf16[1,256,512]{2,1,0:T(8,128)(2,1)} %image.1, bf16[3,3,256,1024]{3,2,1,0:T(8,128)(2,1)} %weight.1, f32[1,256]{1,0:T(1,128)} %bitcast.2, ...), custom_call_target="tpu_custom_call" | custom-call | tf_op jit(solution)/shard_map/gather/pallas_call | solution.py:732
  39.8 3.2 %finish.1 = (f32[3,3,256,512]{3,2,1,0:T(8,128)}, f32[1,256]{1,0:T(1,128)}, bf16[1,1024,128]{2,1,0:T(8,128)(2,1)}) custom-call(bf16[10,256,512]{2,1,0:T(8,128)(2,1)S(1)} %get-tuple-element.11.rows, bf16[3,256,2048]{2,1,0:T(8,128)(2,1)S(1)} %get-tuple-element.12.grads, f32[9,256,512]{2,1,0:T(8,128)S(1)} %get-tuple-element.13.gw_own, ...), custom_call_target="tpu_custom_call" | custom-call | tf_op jit(solution)/shard_map/finish/pallas_call | solution.py:775

commit v5 on v4

--- a/solution.py
+++ b/solution.py
@@ -23,8 +23,10 @@
     return pl.ds(pl.multiple_of(q * cols, cols), count * cols)
 
 
-def store_shifts(grads, place, grad):
+def store_shifts(grads, gb_own, place, grad):
     wide = grad.astype(jnp.float32)
+    width = gb_own.shape[1]
+    gb_own[...] += sum(wide[:, k:k + width] for k in range(0, wide.shape[1], width))
     grads[0, :, place] = shift_cols(wide, 1).astype(jnp.bfloat16)
     grads[2, :, place] = shift_cols(wide, -1).astype(jnp.bfloat16)
 
@@ -35,13 +37,6 @@
     window = rows[pl.ds(start + a, count)].reshape(count * cols, depth)
     left = grads[:, :, lanes(start, cols, count)].reshape(3 * o, count * cols)
     return jnp.dot(left, window, preferred_element_type=jnp.float32).reshape(3, o, depth)
-
-
-def bias_tap(grads, cols, start, count):
-    ones = jnp.ones((8, count * cols), jnp.bfloat16)
-    return lax.dot_general(
-        ones, grads[1, :, lanes(start, cols, count)], NT, preferred_element_type=jnp.float32
-    )
 
 
 def late_row(block, n_f):
@@ -80,16 +75,6 @@
     bound_at = jnp.maximum(last - dist, jnp.maximum(dist + 1, 2))
     near = n_f // 2
 
-    def down_row(block):
-        return jnp.where(block == 0, last - 1, last)
-
-    def up_row(block):
-        return jnp.where(block == 0, 0, 1)
-
-    def relayed(q, block):
-        down, up = down_row(block), up_row(block)
-        return ((q == down) & (p < down)) | ((q == up) & (p > up))
-
     load_row = pltpu.make_async_copy(image.at[0], rows.at[1 + first + p], load_sem.at[0])
     load_w = pltpu.make_async_copy(
         weight.at[:, :, :, pl.ds(pl.multiple_of(c * depth, depth), depth)], w, load_sem.at[1]
@@ -137,8 +122,6 @@
         row_copy(q, h, "filt", p, row_send.at[0, 0, 0]).wait_recv()
 
     def crosses(q, h):
-        if pair:
-            return jnp.logical_not(relayed(q, s))
         return ((q > 0) & (q < last)) | (q == p) | (h == 0)
 
     def pass_on(q, h, right, left):
@@ -211,7 +194,7 @@
         def _(k):
             gw_own[k] = jnp.zeros((o, depth), jnp.float32)
 
-        gb_own[...] = jnp.zeros(gb_own.shape, jnp.float32)
+    gb_own[...] = jnp.zeros(gb_own.shape, jnp.float32)
 
     def add_tap(q, a, r):
         sums = lax.dot_general(
@@ -291,6 +274,13 @@
             s == n_s - 1, jnp.maximum(last - p, 1), jnp.maximum(last - p, p + 1)
         )
         return jnp.where(r == 0, low, jnp.where(r == last, high, jnp.abs(r - p) + 1))
+
+    def finished_at(r):
+        if not pair:
+            return done_at(r)
+        return jnp.where(
+            (dist > 0) & (done_at(r) < last - dist), done_at(r) + 1, done_at(r)
+        )
 
     def sends_grad(r):
         return early | (r != own_bound) if pair else r >= 0
@@ -315,11 +305,11 @@
                 g_copy(first + r, d).start()
 
         send_out(r)
-        store_shifts(grads, lanes(first + r, cols), grad)
+        store_shifts(grads, gb_own, lanes(first + r, cols), grad)
 
     def finish_bound():
         grad, _ = activate(bound)
-        store_shifts(grads, lanes(first + bound, cols), grad)
+        store_shifts(grads, gb_own, lanes(first + bound, cols), grad)
 
     def send_out(r):
         @pl.when(r == p)
@@ -334,39 +324,7 @@
     load_cot.wait()
     load_bias.wait()
 
-    def relay_pair(t):
-        down, up = down_row(other), up_row(other)
-
-        @pl.when((p <= down) & (t == jnp.where(p == down, 1, n_f - p)))
-        def _():
-            for h in range(2):
-                wait_row(other * n_f + down, h)
-
-                @pl.when(p > 0)
-                def _():
-                    to_left(other * n_f + down, h).start()
-
-        @pl.when((p >= up) & (t == jnp.where(p == up, 1, p + 1)))
-        def _():
-            for h in range(2):
-                wait_row(other * n_f + up, h)
-
-                @pl.when(p < last)
-                def _():
-                    to_right(other * n_f + up, h).start()
-
-    def arrive(q):
-        down, up = down_row(other), up_row(other)
-
-        @pl.when(jnp.logical_not(((q == down) & (p <= down)) | ((q == up) & (p >= up))))
-        def _():
-            for h in range(2):
-                wait_row(other * n_f + q, h)
-
     def relay(t):
-        if pair:
-            return relay_pair(t)
-
         @pl.when(t == p + 1)
         def _():
             for block in x_peers:
@@ -376,8 +334,6 @@
                 def _():
                     to_right(block * n_f, 1).start()
 
-                wait_row(block * n_f, 0)
-
         @pl.when(t == n_f - p)
         def _():
             for block in x_peers:
@@ -387,6 +343,15 @@
                 def _():
                     to_left(block * n_f + last, 1).start()
 
+    def settle(t):
+        @pl.when(t == p + 1)
+        def _():
+            for block in x_peers:
+                wait_row(block * n_f, 0)
+
+        @pl.when(t == n_f - p)
+        def _():
+            for block in x_peers:
                 wait_row(block * n_f + last, 0)
 
     def add_edges(t):
@@ -397,7 +362,6 @@
 
             @pl.when(t == jnp.where(early, dist + 1, n_f - dist))
             def _():
-                arrive(edge - other * n_f)
                 add_tap(edge, tap, own_bound)
 
             @pl.when(early & (t == dist + 1))
@@ -406,7 +370,8 @@
 
             @pl.when(early & (t == jnp.maximum(dist + 1, 2)))
             def _():
-                arrive(after - other * n_f)
+                for h in range(2):
+                    wait_row(after, h)
                 add_tap(after, tap, bound)
 
             return
@@ -434,7 +399,7 @@
     def finish_rows(t):
         @pl.loop(0, n_f)
         def _(r):
-            @pl.when(done_at(r) == t)
+            @pl.when(finished_at(r) == t)
             def _():
                 finish(r)
 
@@ -445,9 +410,6 @@
 
     def add_rows(a, start, count):
         gw_own[3 * a:3 * a + 3] += rows_tap(rows, grads, a, start, count)
-
-    def add_bias(start, count):
-        gb_own[...] += bias_tap(grads, cols, start, count)
 
     def share_grad(q):
         g_copy(q, 0).wait_recv()
@@ -456,12 +418,11 @@
     def take_grad(q):
         h_copy(q, sibling).wait_recv()
         place = lanes(q, cols)
-        store_shifts(grads, place, grads[1, :, place])
+        store_shifts(grads, gb_own, place, grads[1, :, place])
 
     def add_all(start, count):
         for a in range(3):
             add_rows(a, start, count)
-        add_bias(start, count)
 
     def near_rows():
         @pl.when(early)
@@ -471,6 +432,9 @@
         @pl.when(late)
         def _():
             add_all(first + jnp.where(low, 1, n_f - near), near - 1)
+
+    def far_rows():
+        add_all(first + jnp.where(low, near, 0), n_f - near)
 
     def tail_of_pair():
         def place(k):
@@ -483,62 +447,64 @@
 
         @pl.when(late)
         def _():
+            share_grad(place(0))
+
+        @pl.when(dist == 0)
+        def _():
+            far_rows()
+
+        @pl.loop(1, near)
+        def _(k):
+            share_grad(place(k))
+
+        @pl.when(early)
+        def _():
+            cot_share(sibling).wait_recv()
+            finish_bound()
+
+        relay(n_f)
+        settle(n_f)
+
+        @pl.when(late)
+        def _():
             add_edges(n_f)
             start_sums(n_f)
-
-        add_all(first + jnp.where(low, near, 0), n_f - near)
-
-        @pl.when(early)
-        def _():
-            share_grad(place(1))
-            cot_share(sibling).wait_recv()
-            finish_bound()
-
-            @pl.loop(2, last)
-            def _(k):
-                arrive(place(k) - other * n_f)
-
-        @pl.when(late)
-        def _():
-            finish_rows(n_f)
-            share_grad(place(0))
-            share_grad(place(1))
-            add_all(first + own_bound, 1)
-
-            @pl.loop(0, last - 1)
-            def _(k):
-                arrive(place(k) - other * n_f)
-
             take_grad(place(0))
-
-        @pl.loop(2, near)
-        def _(k):
-            share_grad(place(k))
+            for h in range(2):
+                wait_row(place(1), h)
 
         @pl.loop(1, near)
         def _(k):
             take_grad(place(k))
 
-        relay(n_f)
+        @pl.loop(2, last)
+        def _(k):
+            for h in range(2):
+                wait_row(place(k), h)
+
         add_all(other * n_f + jnp.where(low, 0, n_f - near), near)
+
+        @pl.when(late)
+        def _():
+            finish_rows(n_f)
+            add_all(first + own_bound, 1)
 
         @pl.loop(near, n_f)
         def _(k):
             share_grad(place(k))
+
+        @pl.loop(near, n_f)
+        def _(k):
             take_grad(place(k))
-
-            @pl.when(k < last)
-            def _():
-                add_all(place(k), 1)
 
     def tail_of_many():
         relay(n_f)
+        settle(n_f)
         add_edges(n_f)
         start_sums(n_f)
         finish_rows(n_f)
         for a in range(3):
             own_rows(a)
-        gb_own[...] = bias_tap(grads, cols, own_start, n_f - 1)
 
         for block in x_peers:
             start = early_row(block, n_f)
@@ -559,7 +525,6 @@
             for a in range(3):
                 add_rows(a, start, n_f - 1)
 
-            add_bias(start, n_f - 1)
 
         for block in x_peers:
             share_grad(late_row(block, n_f))
@@ -580,6 +545,14 @@
 
         relay(t)
 
+        if pair:
+            @pl.when((t == last) & (dist > 0))
+            def _():
+                near_rows()
+                far_rows()
+
+        settle(t)
+
         @pl.when(p - t >= 0)
         def _():
             add_row(p - t)
@@ -599,7 +572,7 @@
         finish_rows(t)
 
         if pair:
-            @pl.when(t == n_f - 2)
+            @pl.when((t == n_f - 2) & (dist == 0))
             def _():
                 near_rows()
 
@@ -645,17 +618,6 @@
         def _():
             for h in range(2):
                 to_left(first + r, h).wait_send()
-
-    if pair:
-        @pl.when((p <= down_row(other)) & (p > 0))
-        def _():
-            for h in range(2):
-                to_left(other * n_f + down_row(other), h).wait_send()
-
-        @pl.when((p >= up_row(other)) & (p < last))
-        def _():
-            for h in range(2):
-                to_right(other * n_f + up_row(other), h).wait_send()
 
     for block in x_peers:
         @pl.loop(0, n_f)
@@ -667,14 +629,13 @@
             else:
                 h_copy(block * n_f + q, c).wait_send()
 
-        if not pair:
-            @pl.when(p < last)
-            def _():
-                to_right(block * n_f, 1).wait_send()
-
-            @pl.when(p > 0)
-            def _():
-                to_left(block * n_f + last, 1).wait_send()
+        @pl.when(p < last)
+        def _():
+            to_right(block * n_f, 1).wait_send()
+
+        @pl.when(p > 0)
+        def _():
+            to_left(block * n_f + last, 1).wait_send()
 
     if pair:
         @pl.when(early)
@@ -694,17 +655,14 @@
 
     if n_s == 2:
         p, s = lax.axis_index("filt"), lax.axis_index("sp")
-        late = [((1 - s) * n_f + jnp.where(p < n_f // 2, n_f - 1, 0), 1)]
+        late = [((1 - s) * n_f + jnp.where(p < n_f // 2, n_f // 2, 0), n_f - n_f // 2)]
     else:
         late = [(n_f - 1, 2)] + [(block * n_f, 1) for block in range(2, n_s)]
 
     def gw_copy(k):
         return pltpu.make_async_copy(total.at[k], gw.at[k // 3, k % 3], sem.at[k])
 
-    bias = gb_own[...]
-    for start, count in late:
-        bias = bias + bias_tap(grads, cols, start, count)
-    gb[...] = bias[:1]
+    gb[...] = jnp.sum(gb_own[...].T, axis=0, keepdims=True)
 
     for a in range(3):
         value = gw_own[3 * a:3 * a + 3]
@@ -735,7 +693,7 @@
             pltpu.VMEM((total + 2, cols, depth), jnp.bfloat16),
             pltpu.VMEM((3, o, total * cols), jnp.bfloat16),
             pltpu.VMEM((9, o, depth), jnp.float32),
-            pltpu.VMEM((8, o), jnp.float32),
+            pltpu.VMEM((o, 128), jnp.float32),
             pltpu.VMEM((n_f * o, cols // n_in), jnp.bfloat16),
         ),
         in_specs=[hbm, hbm, hbm, hbm],

time: 43.3 us -> 37 us (0.85)
  the two profiles are of different devices: /device:TPU:1 before, /device:TPU:17 now
where the time goes in v5:
time: 37 us; the launch traced here: 36.9 us
  Pallas kernels  36.3 us (98%)
  between operations  0.64 us (2%)
    pallas_call x1, Pallas kernels, on_device(): pl.pallas_call(functools.partial(gather_kernel, n_f, n_s), out_shape=(plt...  33 us
    pallas_call x1, Pallas kernels, on_device(): pl.pallas_call(functools.partial(finish_kernel, n_f, n_s), out_shape=(jax...  3.27 us

profile of v5, /device:TPU:17, one launch (start us, length us, event | category | flops | bytes accessed | tf_op | source)
XLA Modules:
  0.0 36.9 jit_solution(13119868078173752776)
XLA Ops:
  0.6 33.0 %gather.1 = (bf16[10,256,512]{2,1,0:T(8,128)(2,1)S(1)}, bf16[3,256,2048]{2,1,0:T(8,128)(2,1)S(1)}, f32[9,256,512]{2,1,0:T(8,128)S(1)}, f32[256,128]{1,0:T(8,128)S(1)}, bf16[1024,128]{1,0:T(8,128)(2,1)S(1)}) custom-call(bf16[1,256,512]{2,1,0:T(8,128)(2,1)} %image.1, bf16[3,3,256,1024]{3,2,1,0:T(8,128)(2,1)} %weight.1, f32[1,256]{1,0:T(1,128)} %bitcast.2, ...), custom_call_target="tpu_custom_call" | custom-call | tf_op jit(solution)/shard_map/gather/pallas_call | solution.py:690
  33.6 3.3 %finish.1 = (f32[3,3,256,512]{3,2,1,0:T(8,128)}, f32[1,256]{1,0:T(1,128)}, bf16[1,1024,128]{2,1,0:T(8,128)(2,1)}) custom-call(bf16[10,256,512]{2,1,0:T(8,128)(2,1)S(1)} %get-tuple-element.11.rows, bf16[3,256,2048]{2,1,0:T(8,128)(2,1)S(1)} %get-tuple-element.12.grads, f32[9,256,512]{2,1,0:T(8,128)S(1)} %get-tuple-element.13.gw_own, ...), custom_call_target="tpu_custom_call" | custom-call | tf_op jit(solution)/shard_map/finish/pallas_call | solution.py:733

commit v6 on v5

--- a/solution.py
+++ b/solution.py
@@ -81,11 +81,6 @@
     )
     load_cot = pltpu.make_async_copy(cotangent, cot.at[pl.ds(1, n_f)], load_sem.at[2])
     load_bias = pltpu.make_async_copy(bias_in, bias, load_sem.at[3])
-    load_row.start()
-    load_w.start()
-    load_cot.start()
-    load_bias.start()
-
     barrier = pltpu.get_barrier_semaphore()
 
     @pl.when(p < last)
@@ -100,10 +95,13 @@
     pl.semaphore_signal(barrier, 1, device_id={"in": sibling}, device_id_type=MESH)
     pl.semaphore_wait(barrier, 1 + s + jnp.where(p > 0, 1, 0))
 
-    piece = cols // 2
+    cut = cols * 7 // 16
+
+    def span(h):
+        return pl.ds(0, cut) if h == 0 else pl.ds(cut, cols - cut)
 
     def row_copy(q, h, way, where, send):
-        slot = rows.at[1 + q, pl.ds(h * piece, piece)]
+        slot = rows.at[1 + q, span(h)]
         return pltpu.make_async_remote_copy(
             src_ref=slot, dst_ref=slot, send_sem=send, recv_sem=row_recv.at[q, h],
             device_id={way: where}, device_id_type=MESH,
@@ -140,7 +138,7 @@
                 to_x(q, h, d).start()
 
     def own_copy(h, way, where, send):
-        place = pl.ds(h * piece, piece)
+        place = span(h)
         return pltpu.make_async_remote_copy(
             src_ref=image.at[0, place], dst_ref=rows.at[1 + first + p, place],
             send_sem=send, recv_sem=row_recv.at[first + p, h],
@@ -165,6 +163,11 @@
         @pl.when(peer_s < s)
         def _():
             pl.semaphore_signal(ready_x, 1, device_id={"sp": peer_s}, device_id_type=MESH)
+
+    load_row.start()
+    load_w.start()
+    load_cot.start()
+    load_bias.start()
 
     @pl.when(p < last)
     def _():

time: 37 us -> 36.7 us (level)
  the two profiles are of different devices: /device:TPU:17 before, /device:TPU:1 now
where the time goes in v6:
time: 36.7 us; the launch traced here: 36.5 us
  Pallas kernels  35.9 us (98%)
  between operations  0.64 us (2%)
    pallas_call x1, Pallas kernels, on_device(): pl.pallas_call(functools.partial(gather_kernel, n_f, n_s), out_shape=(plt...  32.6 us
    pallas_call x1, Pallas kernels, on_device(): pl.pallas_call(functools.partial(finish_kernel, n_f, n_s), out_shape=(jax...  3.27 us

profile of v6, /device:TPU:1, one launch (start us, length us, event | category | flops | bytes accessed | tf_op | source)
XLA Modules:
  0.0 36.5 jit_solution(14649121086295975371)
XLA Ops:
  0.6 32.6 %gather.1 = (bf16[10,256,512]{2,1,0:T(8,128)(2,1)S(1)}, bf16[3,256,2048]{2,1,0:T(8,128)(2,1)S(1)}, f32[9,256,512]{2,1,0:T(8,128)S(1)}, f32[256,128]{1,0:T(8,128)S(1)}, bf16[1024,128]{1,0:T(8,128)(2,1)S(1)}) custom-call(bf16[1,256,512]{2,1,0:T(8,128)(2,1)} %image.1, bf16[3,3,256,1024]{3,2,1,0:T(8,128)(2,1)} %weight.1, f32[1,256]{1,0:T(1,128)} %bitcast.2, ...), custom_call_target="tpu_custom_call" | custom-call | tf_op jit(solution)/shard_map/gather/pallas_call | solution.py:693
  33.2 3.3 %finish.1 = (f32[3,3,256,512]{3,2,1,0:T(8,128)}, f32[1,256]{1,0:T(1,128)}, bf16[1,1024,128]{2,1,0:T(8,128)(2,1)}) custom-call(bf16[10,256,512]{2,1,0:T(8,128)(2,1)S(1)} %get-tuple-element.11.rows, bf16[3,256,2048]{2,1,0:T(8,128)(2,1)S(1)} %get-tuple-element.12.grads, f32[9,256,512]{2,1,0:T(8,128)S(1)} %get-tuple-element.13.gw_own, ...), custom_call_target="tpu_custom_call" | custom-call | tf_op jit(solution)/shard_map/finish/pallas_call | solution.py:736

commit v7 on v6

--- a/solution.py
+++ b/solution.py
@@ -95,13 +95,10 @@
     pl.semaphore_signal(barrier, 1, device_id={"in": sibling}, device_id_type=MESH)
     pl.semaphore_wait(barrier, 1 + s + jnp.where(p > 0, 1, 0))
 
-    cut = cols * 7 // 16
-
-    def span(h):
-        return pl.ds(0, cut) if h == 0 else pl.ds(cut, cols - cut)
+    piece = cols // 2
 
     def row_copy(q, h, way, where, send):
-        slot = rows.at[1 + q, span(h)]
+        slot = rows.at[1 + q, pl.ds(h * piece, piece)]
         return pltpu.make_async_remote_copy(
             src_ref=slot, dst_ref=slot, send_sem=send, recv_sem=row_recv.at[q, h],
             device_id={way: where}, device_id_type=MESH,
@@ -138,7 +135,7 @@
                 to_x(q, h, d).start()
 
     def own_copy(h, way, where, send):
-        place = span(h)
+        place = pl.ds(h * piece, piece)
         return pltpu.make_async_remote_copy(
             src_ref=image.at[0, place], dst_ref=rows.at[1 + first + p, place],
             send_sem=send, recv_sem=row_recv.at[first + p, h],
@@ -490,11 +487,14 @@
         @pl.when(late)
         def _():
             finish_rows(n_f)
-            add_all(first + own_bound, 1)
 
         @pl.loop(near, n_f)
         def _(k):
             share_grad(place(k))
+
+        @pl.when(late)
+        def _():
+            add_all(first + own_bound, 1)
 
         @pl.loop(near, n_f)
         def _(k):

time: 36.7 us -> 36.3 us (0.989)
  Pallas kernels: 35.9 us -> 35.3 us
    pallas_call x1, Pallas kernels: 32.6 us -> 32 us  [on_device(): pl.pallas_call(functools.partial(gather_kernel, n_f, n_s), out_shape=(plt...]
where the time goes in v7:
time: 36.3 us; the launch traced here: 36 us
  Pallas kernels  35.3 us (97%)
  between operations  0.64 us (2%)
    pallas_call x1, Pallas kernels, on_device(): pl.pallas_call(functools.partial(gather_kernel, n_f, n_s), out_shape=(plt...  32 us
    pallas_call x1, Pallas kernels, on_device(): pl.pallas_call(functools.partial(finish_kernel, n_f, n_s), out_shape=(jax...  3.27 us

profile of v7, /device:TPU:1, one launch (start us, length us, event | category | flops | bytes accessed | tf_op | source)
XLA Modules:
  0.0 36.0 jit_solution(10597924773687298580)
XLA Ops:
  0.6 32.0 %gather.1 = (bf16[10,256,512]{2,1,0:T(8,128)(2,1)S(1)}, bf16[3,256,2048]{2,1,0:T(8,128)(2,1)S(1)}, f32[9,256,512]{2,1,0:T(8,128)S(1)}, f32[256,128]{1,0:T(8,128)S(1)}, bf16[1024,128]{1,0:T(8,128)(2,1)S(1)}) custom-call(bf16[1,256,512]{2,1,0:T(8,128)(2,1)} %image.1, bf16[3,3,256,1024]{3,2,1,0:T(8,128)(2,1)} %weight.1, f32[1,256]{1,0:T(1,128)} %bitcast.2, ...), custom_call_target="tpu_custom_call" | custom-call | tf_op jit(solution)/shard_map/gather/pallas_call | solution.py:693
  32.7 3.3 %finish.1 = (f32[3,3,256,512]{3,2,1,0:T(8,128)}, f32[1,256]{1,0:T(1,128)}, bf16[1,1024,128]{2,1,0:T(8,128)(2,1)}) custom-call(bf16[10,256,512]{2,1,0:T(8,128)(2,1)S(1)} %get-tuple-element.11.rows, bf16[3,256,2048]{2,1,0:T(8,128)(2,1)S(1)} %get-tuple-element.12.grads, f32[9,256,512]{2,1,0:T(8,128)S(1)} %get-tuple-element.13.gw_own, ...), custom_call_target="tpu_custom_call" | custom-call | tf_op jit(solution)/shard_map/finish/pallas_call | solution.py:736

commit v8 on v6

--- a/solution.py
+++ b/solution.py
@@ -95,7 +95,7 @@
     pl.semaphore_signal(barrier, 1, device_id={"in": sibling}, device_id_type=MESH)
     pl.semaphore_wait(barrier, 1 + s + jnp.where(p > 0, 1, 0))
 
-    cut = cols * 7 // 16
+    cut = cols * 3 // 8
 
     def span(h):
         return pl.ds(0, cut) if h == 0 else pl.ds(cut, cols - cut)
@@ -490,11 +490,14 @@
         @pl.when(late)
         def _():
             finish_rows(n_f)
-            add_all(first + own_bound, 1)
 
         @pl.loop(near, n_f)
         def _(k):
             share_grad(place(k))
+
+        @pl.when(late)
+        def _():
+            add_all(first + own_bound, 1)
 
         @pl.loop(near, n_f)
         def _(k):
@@ -665,8 +668,6 @@
     def gw_copy(k):
         return pltpu.make_async_copy(total.at[k], gw.at[k // 3, k % 3], sem.at[k])
 
-    gb[...] = jnp.sum(gb_own[...].T, axis=0, keepdims=True)
-
     for a in range(3):
         value = gw_own[3 * a:3 * a + 3]
         for start, count in late:
@@ -674,6 +675,8 @@
         for b in range(3):
             total[3 * a + b] = value[b]
             gw_copy(3 * a + b).start()
+
+    gb[...] = jnp.sum(gb_own[...].T, axis=0, keepdims=True)
 
     for k in range(9):
         gw_copy(k).wait()

time: 36.7 us -> 36.5 us (level); the launches traced: 36.5 us -> 35.8 us
  Pallas kernels: 35.9 us -> 35.2 us
    pallas_call x1, Pallas kernels: 32.6 us -> 31.9 us  [on_device(): pl.pallas_call(functools.partial(gather_kernel, n_f, n_s), out_shape=(plt...]
where the time goes in v8:
time: 36.5 us; the launch traced here: 35.8 us
  Pallas kernels  35.2 us (96%)
  between operations  0.64 us (2%)
    pallas_call x1, Pallas kernels, on_device(): pl.pallas_call(functools.partial(gather_kernel, n_f, n_s), out_shape=(plt...  31.9 us
    pallas_call x1, Pallas kernels, on_device(): pl.pallas_call(functools.partial(finish_kernel, n_f, n_s), out_shape=(jax...  3.27 us

profile of v8, /device:TPU:1, one launch (start us, length us, event | category | flops | bytes accessed | tf_op | source)
XLA Modules:
  0.0 35.8 jit_solution(2093718062865971173)
XLA Ops:
  0.6 31.9 %gather.1 = (bf16[10,256,512]{2,1,0:T(8,128)(2,1)S(1)}, bf16[3,256,2048]{2,1,0:T(8,128)(2,1)S(1)}, f32[9,256,512]{2,1,0:T(8,128)S(1)}, f32[256,128]{1,0:T(8,128)S(1)}, bf16[1024,128]{1,0:T(8,128)(2,1)S(1)}) custom-call(bf16[1,256,512]{2,1,0:T(8,128)(2,1)} %image.1, bf16[3,3,256,1024]{3,2,1,0:T(8,128)(2,1)} %weight.1, f32[1,256]{1,0:T(1,128)} %bitcast.2, ...), custom_call_target="tpu_custom_call" | custom-call | tf_op jit(solution)/shard_map/gather/pallas_call | solution.py:696
  32.6 3.3 %finish.1 = (f32[3,3,256,512]{3,2,1,0:T(8,128)}, f32[1,256]{1,0:T(1,128)}, bf16[1,1024,128]{2,1,0:T(8,128)(2,1)}) custom-call(bf16[10,256,512]{2,1,0:T(8,128)(2,1)S(1)} %get-tuple-element.11.rows, bf16[3,256,2048]{2,1,0:T(8,128)(2,1)S(1)} %get-tuple-element.12.grads, f32[9,256,512]{2,1,0:T(8,128)S(1)} %get-tuple-element.13.gw_own, ...), custom_call_target="tpu_custom_call" | custom-call | tf_op jit(solution)/shard_map/finish/pallas_call | solution.py:739
